TPU v7x, 32 devices: a whole 2x2x4 slice. The times are simulated.
32 devices in a mesh: row: 8 (over z, y), col: 4 (over x, core).
Axes of the slice: x: 2, y: 2, z: 4, core: 2. Of those that a mesh axis runs over, the one named last changes fastest.
Arguments:
- image_states: bfloat16 [64, 3072], P(('row', 'col')), may hold values from -6 to 6
- latent: float32 [64, 64], P(('row', 'col')), may hold values from -6 to 6
- text_keys: bfloat16 [1024, 3072], P('row', 'col')
- text_values: bfloat16 [1024, 3072], P('row', 'col'), may hold values from -6 to 6
- mod_table: float32 [4, 8, 3072], replicated, may hold values from -3 to 3
- timestep: int32 [4], replicated, may hold values from 0 to 3
- grid_size: int32 [4, 2], replicated, may hold values from 1 to 8, as said below
- rope_offset: int32 [4, 2], replicated, may hold values from 0 to 63
- w_qkv: bfloat16 [3072, 9216], P(None, 'row'), may hold values from -0.109375 to 0.109375
- q_gain: float32 [128], replicated, may hold values from 0.1 to 1.9
- k_gain: float32 [128], replicated, may hold values from 0.5 to 4
- w_out: bfloat16 [3072, 3072], P('col', 'row'), may hold values from -0.109375 to 0.109375
- w_fc1: bfloat16 [3072, 12288], P(None, 'row'), may hold values from -0.109375 to 0.109375
- w_fc2: bfloat16 [12288, 3072], P('row'), may hold values from -0.0546875 to 0.0546875
- w_final: bfloat16 [3072, 64], replicated, may hold values from -0.109375 to 0.109375
Outputs:
- velocity: float32 [64, 64], P(('row', 'col'))
- next_latent: float32 [64, 64], P(('row', 'col'))
Inputs may be any that keep to these rules, and one draw needn't show every extreme that they name: `grid_size`: column 0 is a request's grid height, at most 2; column 1 its grid width, at most 8; in every draw some request has height 2 and some request width 8.
All inputs are finite; a program needn't handle non-finite values.
Results may differ from a plain program's by a relative error of at most 0.008.
Values may be sent and summed in bfloat16 or wider, within the bound.
No kernel may reach another device: no remote copies, remote signals or barrier semaphores. Data moves between devices by JAX's collectives and lax.ppermute only.
A program may use at most 128 MiB of HBM per device.

v0:
```python
import jax
import jax.numpy as jnp
from jax import lax
from jax.sharding import PartitionSpec as P

REQ = 4
TXT = 256
STEPS = 4
eps_norm = 1e-06
blend = 0.25
mask_floor = -1e30


def with_halo(cells, sides, width):
    for axis, dim in sides:
        count = lax.axis_size(axis)
        ends = count - 1
        head = lax.slice_in_dim(cells, 0, width, axis=dim)
        tail = lax.slice_in_dim(cells, cells.shape[dim] - width, cells.shape[dim], axis=dim)
        cells = jnp.concatenate(
            [
                lax.ppermute(tail, axis, [(i, (i + 1) % count) for i in range(ends)]),
                cells,
                lax.ppermute(head, axis, [((i + 1) % count, i) for i in range(ends)]),
            ],
            axis=dim,
        )
    return cells


def layer_norm(values):
    mean_value = jnp.mean(values, -1, keepdims=True)
    centred = values - mean_value
    return centred * lax.rsqrt(jnp.mean(centred * centred, -1, keepdims=True) + eps_norm)


def modulate(values, shift_vec, scale_vec):
    return (layer_norm(values) * (1.0 + scale_vec) + shift_vec).astype(jnp.bfloat16)


def rope_tables(pos_h, pos_w, head_size):
    time_half = head_size // 16
    axis_dim = (head_size - head_size // 8) // 2
    freq_index = jnp.arange(axis_dim // 2, dtype=jnp.float32)
    frequency = 10000.0 ** (-2.0 * freq_index / axis_dim)
    angles = jnp.concatenate(
        [
            jnp.zeros((pos_h.shape[0], time_half), jnp.float32),
            pos_h[:, None] * frequency[None, :],
            pos_w[:, None] * frequency[None, :],
        ],
        1,
    )
    return (jnp.cos(angles), jnp.sin(angles))


def norm_rope(values, gain_vec, cosine_table, sine_table, head_count, head_size):
    row_total = values.shape[0]
    per_head = values.astype(jnp.float32).reshape(row_total, head_count, head_size)
    per_head = (
        per_head * lax.rsqrt(jnp.mean(per_head * per_head, -1, keepdims=True) + eps_norm) * gain_vec
    )
    paired = per_head.reshape(row_total, head_count, head_size // 2, 2)
    even_part = paired[..., 0]
    odd_part = paired[..., 1]
    cos_wide = cosine_table[:, None, :]
    sin_wide = sine_table[:, None, :]
    turned = jnp.stack(
        [even_part * cos_wide - odd_part * sin_wide, even_part * sin_wide + odd_part * cos_wide], -1
    )
    return turned.reshape(row_total, head_count * head_size).astype(jnp.bfloat16)


def on_device(
    image_states,
    latent,
    text_keys,
    text_values,
    mod_table,
    timestep,
    grid_size,
    rope_offset,
    w_qkv,
    q_gain,
    k_gain,
    w_out,
    w_fc1,
    w_fc2,
    w_final,
):
    col_total = lax.axis_size("col")
    row_pos = lax.axis_index("row")
    col_pos = lax.axis_index("col")
    tile_w = image_states.shape[0]
    width = image_states.shape[1]
    head_size = q_gain.shape[0]
    head_count = width // head_size
    local_heads = head_count // col_total
    request = row_pos % REQ
    grid_row = row_pos // REQ
    grid_col = col_pos * tile_w + jnp.arange(tile_w, dtype=jnp.int32)
    req_slots = jnp.arange(REQ, dtype=jnp.int32)
    req_onehot = req_slots == request
    limits = jnp.sum(jnp.where(req_onehot[:, None], grid_size, 0), 0)
    offsets = jnp.sum(jnp.where(req_onehot[:, None], rope_offset, 0), 0)
    step_now = jnp.sum(jnp.where(req_onehot, timestep, 0))
    token_ok = (grid_row < limits[0]) & (grid_col < limits[1])
    modulation = lax.dynamic_index_in_dim(mod_table, step_now, 0, keepdims=False)
    states = image_states.astype(jnp.float32)
    normed = modulate(states, modulation[0], modulation[1])
    joined_cols = jnp.dot(
        lax.all_gather(normed, "row", axis=0, tiled=True), w_qkv, preferred_element_type=jnp.float32
    ).astype(jnp.bfloat16)
    joined = lax.all_to_all(joined_cols, "row", split_axis=0, concat_axis=1, tiled=True)
    pos_h = jnp.zeros((tile_w,), jnp.float32) + (grid_row + offsets[0]).astype(jnp.float32)
    pos_w = (grid_col + offsets[1]).astype(jnp.float32)
    cosine_table, sine_table = rope_tables(pos_h, pos_w, head_size)
    queries = norm_rope(joined[:, :width], q_gain, cosine_table, sine_table, head_count, head_size)
    image_keys = norm_rope(
        joined[:, width : 2 * width], k_gain, cosine_table, sine_table, head_count, head_size
    )
    q_heads, k_heads, v_heads = (
        lax.all_to_all(queries, "col", split_axis=1, concat_axis=0, tiled=True),
        lax.all_to_all(image_keys, "col", split_axis=1, concat_axis=0, tiled=True),
        lax.all_to_all(joined[:, 2 * width :], "col", split_axis=1, concat_axis=0, tiled=True),
    )
    image_rows = k_heads.shape[0]
    text_rows = text_keys.shape[0]
    shard_rows = image_rows + text_rows
    q_block = q_heads.reshape(image_rows, local_heads, head_size)
    key_rows = jnp.concatenate([k_heads, text_keys], 0)
    value_rows = jnp.concatenate([v_heads, text_values], 0)
    run_max = jnp.full((image_rows, local_heads), mask_floor, jnp.float32)
    key_piece = lax.all_gather(key_rows, "row", axis=0, tiled=True)
    value_piece = lax.all_gather(value_rows, "row", axis=0, tiled=True)
    piece_rows = key_piece.shape[0]
    global_row = jnp.arange(piece_rows, dtype=jnp.int32)
    shard_id = global_row // shard_rows
    within = global_row % shard_rows
    is_image = within < image_rows
    source_col = within // tile_w
    source_cell = within % tile_w
    image_req = shard_id % REQ
    text_req = (shard_id * text_rows + within - image_rows) // TXT
    key_req = jnp.where(is_image, image_req, text_req)
    key_onehot = key_req[:, None] == req_slots[None, :]
    key_height = jnp.sum(jnp.where(key_onehot, grid_size[:, 0][None, :], 0), 1)
    key_width = jnp.sum(jnp.where(key_onehot, grid_size[:, 1][None, :], 0), 1)
    image_ok = (shard_id // REQ < key_height) & (source_col * tile_w + source_cell < key_width)
    key_ok = (key_req == request) & (jnp.logical_not(is_image) | image_ok)
    scores = jnp.einsum(
        "qhd,khd->qhk",
        q_block,
        key_piece.reshape(piece_rows, local_heads, head_size),
        preferred_element_type=jnp.float32,
    ) * head_size ** (-0.5)
    new_max = jnp.maximum(run_max, jnp.max(jnp.where(key_ok, scores, mask_floor), -1))
    weights = jnp.where(key_ok, jnp.exp(scores - new_max[..., None]), 0.0)
    new_sum = jnp.sum(weights, -1)
    new_acc = jnp.einsum(
        "qhk,khd->qhd",
        weights.astype(jnp.bfloat16),
        value_piece.reshape(piece_rows, local_heads, head_size),
        preferred_element_type=jnp.float32,
    )
    mixed = (
        (new_acc / new_sum[..., None])
        .astype(jnp.bfloat16)
        .reshape(image_rows, local_heads * head_size)
    )
    partial_out = jnp.dot(
        mixed, lax.all_gather(w_out, "row", axis=1, tiled=True), preferred_element_type=jnp.float32
    )
    attended = lax.psum_scatter(
        partial_out.astype(jnp.bfloat16), "col", scatter_dimension=0, tiled=True
    ).astype(jnp.float32)
    first_res = (states + modulation[2] * attended).astype(jnp.bfloat16)
    normed_two = modulate(first_res.astype(jnp.float32), modulation[3], modulation[4])
    all_rows = lax.all_gather(normed_two, "row", axis=0, tiled=True)
    hidden = jax.nn.gelu(
        jnp.dot(all_rows, w_fc1, preferred_element_type=jnp.float32), approximate=True
    ).astype(jnp.bfloat16)
    every_term = jnp.dot(hidden, w_fc2, preferred_element_type=jnp.float32)
    every_sum = lax.psum(every_term, "row")
    mlp_out = lax.dynamic_slice_in_dim(every_sum, row_pos * tile_w, tile_w, 0)
    second_res = first_res.astype(jnp.float32) + modulation[5] * mlp_out
    normed_three = modulate(second_res, modulation[6], modulation[7])
    raw_velocity = jnp.dot(normed_three, w_final, preferred_element_type=jnp.float32)
    masked = jnp.where(token_ok[:, None], raw_velocity, 0.0)
    padded = with_halo(masked, (("col", 0),), 1)
    left_side = padded[:-2]
    right_side = padded[2:]
    velocity = jnp.where(
        token_ok[:, None], masked + blend * (left_side + right_side - 2.0 * masked), 0.0
    )
    next_latent = latent + -1.0 / STEPS * velocity
    return (velocity, next_latent)


def solution(mesh):
    placed = (
        P(("row", "col"), None),
        P(("row", "col"), None),
        P("row", "col"),
        P("row", "col"),
        P(),
        P(),
        P(),
        P(),
        P(None, "row"),
        P(),
        P(),
        P("col", "row"),
        P(None, "row"),
        P("row", None),
        P(),
    )
    return jax.shard_map(
        on_device,
        mesh=mesh,
        in_specs=placed,
        out_specs=(P(("row", "col"), None), P(("row", "col"), None)),
        check_vma=False,
    )
```

profile of v0, /device:TPU:1, one launch (start us, length us, event | category | flops | bytes accessed | tf_op | source)
XLA Modules:
  0.0 413.6 jit_solution(1863781639350607465)
XLA Ops:
  12.3 2.2 dynamic-slice_add_fusion
  15.3 25.6 %all-gather = bf16[8,2,3072]{2,1,0:T(2,128)(2,1)S(1)} all-gather(bf16[1,2,3072]{2,1,0:T(2,128)(2,1)S(1)} %fusion.50), channel_id=1, replica_groups=mesh['row'=8,'col'=4] {'row'}, dimensions={0}, use_global_device_ids=true | all-gather | bytes 110592 | tf_op jit(solution)/shard_map/all_gather | solution.py:112
  41.0 4.0 convolution_convert_fusion.1
  45.7 5.0 %all-to-all-start = ((bf16[8,2,1152]{2,1,0:T(2,128)(2,1)}), bf16[8,2,1152]{2,1,0:T(2,128)(2,1)S(1)}, u32[]{:S(2)}, u32[]{:S(2)}) async-start(bf16[8,2,1152]{2,1,0:T(2,128)(2,1)} %all_to_all.50), calls=%async_computation | async-start | bytes 73728 | tf_op jit(solution)/shard_map/all_to_all | solution.py:114
  59.2 2.3 reshape.264
  63.3 5.2 %slice_multiply_fusion.5 = (f32[2,24,64,1]{3,2,1,0:T(8,128)}, f32[2,24,64,1]{3,2,1,0:T(8,128)}, f32[2,24,64,1]{3,2,1,0:T(8,128)}, f32[2,24,64,1]{3,2,1,0:T(8,128...) fusion(f32[2,24,64,2]{3,2,1,0:T(8,128)S(1)} %multiply_multiply_, ...), kind=kLoop, calls=%fused_computation.11 | loop fusion | flops 24576 | bytes 148480 | tf_op jit(solution)/shard_map/mul | solution.py:69
  68.5 2.5 copy.52
  71.1 2.5 copy.53
  73.6 2.5 copy.54
  76.1 2.5 copy.55
  80.8 2.0 copy.56
  82.8 2.1 convert_element_type.69
  84.9 14.5 %all_to_all.67 = bf16[2,4,768]{2,0,1:T(2,128)(2,1)} all-to-all(bf16[2,4,768]{2,0,1:T(2,128)(2,1)S(1)} %copy.57), channel_id=1, replica_groups=mesh['row'=8,'col'=4] {'col'}, dimensions={1} | all-to-all | bytes 24576 | tf_op jit(solution)/shard_map/all_to_all | solution.py:124
  101.8 7.8 %all_to_all.68 = bf16[2,4,768]{2,0,1:T(2,128)(2,1)} all-to-all(bf16[2,4,768]{2,0,1:T(2,128)(2,1)} %bitcast.72), channel_id=1, replica_groups=mesh['row'=8,'col'=4] {'col'}, dimensions={1} | all-to-all | bytes 24576 | tf_op jit(solution)/shard_map/all_to_all | solution.py:125
  112.8 2.5 copy.59
  115.4 2.5 copy.60
  121.9 3.9 all-to-all-start.3
  127.2 2.2 all-to-all-done.3
  129.4 14.7 %all-gather.8.cloned.1.call-done = bf16[1088,768]{1,0:T(8,128)(2,1)} async-done(((bf16[136,768]{1,0:T(8,128)(2,1)}), bf16[1088,768]{1,0:T(8,128)(2,1)}) %all-gather.8.cloned.1.call-update) | async-done | bytes 1671184 | tf_op jit(solution)/shard_map/all_gather | solution.py:134
  144.1 3.8 copy.58
  147.9 42.3 %all-gather.6.cloned.1.call-done = bf16[1088,768]{1,0:T(8,128)(2,1)} async-done(((bf16[136,768]{1,0:T(8,128)(2,1)}), bf16[1088,768]{1,0:T(8,128)(2,1)}) %all-gather.6.cloned.1.call-update) | async-done | bytes 1671184 | tf_op jit(solution)/shard_map/all_gather | solution.py:135
  190.2 2.7 copy.51
  192.9 1.9 select_reduce_fusion
  195.0 77.3 %all-gather.10.cloned.1.call-done = bf16[768,3072]{1,0:T(8,128)(2,1)} async-done(((bf16[768,384]{1,0:T(8,128)(2,1)}), bf16[768,3072]{1,0:T(8,128)(2,1)}) %all-gather.10.cloned.1.call-update) | async-done | bytes 4718608 | tf_op jit(solution)/shard_map/all_gather | solution.py:172
  272.3 3.7 convolution_convert_fusion
  276.0 11.2 %all-reduce = bf16[8,3072]{1,0:T(8,128)(2,1)S(1)} all-reduce(bf16[8,3072]{1,0:T(8,128)(2,1)S(1)} %convolution_convert_fusion), channel_id=2, replica_groups=mesh['row'=8,'col'=4] {'col'}, use_global_device_ids=true, to_apply=%region_11.12.clone | all-reduce | flops 24576 | bytes 98304
  287.7 24.4 %all-gather.1 = bf16[8,2,3072]{2,1,0:T(2,128)(2,1)S(1)} all-gather(bf16[1,2,3072]{2,1,0:T(2,128)(2,1)S(1)} %fusion.51), channel_id=1, replica_groups=mesh['row'=8,'col'=4] {'row'}, dimensions={0}, use_global_device_ids=true | all-gather | bytes 110592 | tf_op jit(solution)/shard_map/all_gather | solution.py:179
  312.2 9.6 %fusion.22 = f32[16,3072]{1,0:T(8,128)} fusion(bf16[1536,3072]{1,0:T(8,128)(2,1)} %param.28, bf16[16,3072]{1,0:T(8,128)(2,1)S(1)} %reshape.272, bf16[3072,1536]{1,0:T(8,128)(2,1)} %param.27), kind=kOutput, calls=%fused_computation.37 | convolution fusion | flops 302211072 | bytes 19169280 | tf_op jit(solution)/shard_map/dot_general | solution.py:183
  323.0 71.4 %all-reduce.3.cloned.1.call-done = f32[16,3072]{1,0:T(8,128)} async-done(((f32[16,3072]{1,0:T(8,128)}), f32[16,3072]{1,0:T(8,128)}) %all-reduce.3.cloned.1.call-update) | async-done | bytes 196624 | tf_op jit(solution)/shard_map/psum | solution.py:184
  396.0 5.6 %collective-permute-start = (f32[1,64]{1,0:T(1,128)S(1)}, f32[1,64]{1,0:T(1,128)S(1)}, u32[]{:S(2)}, u32[]{:S(2)}) collective-permute-start(f32[1,64]{1,0:T(1,128)S(1)} %get-tuple-element.45), channel_id=1, source_target_pairs={{0,1},{1,2},{2,3},{4,5},{5,6},{6,7},{8,9},{9,10},{10,11},{12,13},{... | collective-permute-start | bytes 776 | tf_op jit(solution)/shard_map/ppermute | solution.py:22
  401.5 1.9 collective-permute-start.1
  403.5 2.9 collective-permute-done.1
  (113 shorter events, 30.2 us)
Async XLA Ops:
  7.2 388.5 %copy-start = (bf16[3072,64]{0,1:T(8,128)(2,1)S(1)}, bf16[3072,64]{0,1:T(8,128)(2,1)}, u32[]{:S(2)}) copy-start(bf16[3072,64]{0,1:T(8,128)(2,1)} %param.29) | copy-start | bytes 1179652
  41.0 9.8 %copy-start.12 = (s32[4,2]{0,1:T(2,128)S(1)}, s32[4,2]{0,1:T(2,128)}, u32[]{:S(2)}) copy-start(s32[4,2]{0,1:T(2,128)} %param.21) | copy-start | bytes 100
  41.0 9.8 %copy-start.13 = (s32[4,2]{0,1:T(2,128)S(1)}, s32[4,2]{0,1:T(2,128)}, u32[]{:S(2)}) copy-start(s32[4,2]{0,1:T(2,128)} %param.22) | copy-start | bytes 100
  41.0 12.1 %copy-start.15 = (f32[128]{0:T(128)S(1)}, f32[128]{0:T(128)}, u32[]{:S(2)}) copy-start(f32[128]{0:T(128)} %param.24) | copy-start | bytes 1540
  41.0 12.9 %copy-start.16 = (f32[128]{0:T(128)S(1)}, f32[128]{0:T(128)}, u32[]{:S(2)}) copy-start(f32[128]{0:T(128)} %param.25) | copy-start | bytes 1540
  45.7 10.6 %all-to-all-start = ((bf16[8,2,1152]{2,1,0:T(2,128)(2,1)}), bf16[8,2,1152]{2,1,0:T(2,128)(2,1)S(1)}, u32[]{:S(2)}, u32[]{:S(2)}) async-start(bf16[8,2,1152]{2,1,0:T(2,128)(2,1)} %all_to_all.50), calls=%async_computation | async-start | bytes 73728 | tf_op jit(solution)/shard_map/all_to_all | solution.py:114
  50.7 93.4 %all-gather.8.cloned.1.call-start = ((), (), s32[]{:S(2)}) async-start(), calls=%async_computation.5 | async-start | bytes 1880064 | tf_op jit(solution)/shard_map/all_gather | solution.py:134
  62.2 1.0 copy-start.2
  101.8 88.4 %all-gather.6.cloned.1.call-start = ((), (), s32[]{:S(2)}) async-start(), calls=%async_computation.4 | async-start | bytes 1880064 | tf_op jit(solution)/shard_map/all_gather | solution.py:135
  111.9 160.4 %all-gather.10.cloned.1.call-start = ((), (), s32[]{:S(2)}) async-start(), calls=%async_computation.6 | async-start | bytes 5308416 | tf_op jit(solution)/shard_map/all_gather | solution.py:172
  119.0 0.7 copy-start.3
  119.0 0.8 copy-start.4
  119.0 0.8 copy-start.5
  119.0 6.9 %copy-start.17 = (u32[32]{0:T(128)S(1)}, u32[32]{0:T(128)}, u32[]{:S(2)}) copy-start(u32[32]{0:T(128)} %constant.158) | copy-start | bytes 388
  121.9 7.5 %all-to-all-start.3 = ((bf16[2,4,768]{2,0,1:T(2,128)(2,1)}), bf16[2,4,768]{2,0,1:T(2,128)(2,1)S(1)}, u32[]{:S(2)}, u32[]{:S(2)}) async-start(bf16[2,4,768]{2,0,1:T(2,128)(2,1)} %copy.64), calls=%async_computation.3 | async-start | bytes 24576 | tf_op jit(solution)/shard_map/all_to_all | solution.py:123
  125.9 268.5 %all-reduce.3.cloned.1.call-start = ((), (), s32[]{:S(2)}) async-start(), calls=%async_computation.7 | async-start | bytes 393216 | tf_op jit(solution)/shard_map/psum | solution.py:184
  272.3 14.9 %copy-start.1 = (bf16[2,3072]{1,0:T(2,128)(2,1)S(1)}, bf16[2,3072]{1,0:T(2,128)(2,1)}, u32[]{:S(2)}) copy-start(bf16[2,3072]{1,0:T(2,128)(2,1)} %param.15) | copy-start | bytes 36868
  272.3 14.9 %copy-start.9 = (f32[1,1,3072]{2,1,0:T(1,128)S(1)}, f32[1,1,3072]{2,1,0:T(1,128)}, u32[]{:S(2)}) copy-start(f32[1,1,3072]{2,1,0:T(1,128)} %get-tuple-element.30) | copy-start | bytes 36868
  272.3 15.3 %copy-start.7 = (f32[1,1,3072]{2,1,0:T(1,128)S(1)}, f32[1,1,3072]{2,1,0:T(1,128)}, u32[]{:S(2)}) copy-start(f32[1,1,3072]{2,1,0:T(1,128)} %get-tuple-element.25) | copy-start | bytes 36868
  272.3 15.3 %copy-start.8 = (f32[1,1,3072]{2,1,0:T(1,128)S(1)}, f32[1,1,3072]{2,1,0:T(1,128)}, u32[]{:S(2)}) copy-start(f32[1,1,3072]{2,1,0:T(1,128)} %get-tuple-element.26) | copy-start | bytes 36868
  312.1 82.3 %copy-start.6 = (f32[1,1,3072]{2,1,0:T(1,128)S(1)}, f32[1,1,3072]{2,1,0:T(1,128)}, u32[]{:S(2)}) copy-start(f32[1,1,3072]{2,1,0:T(1,128)} %get-tuple-element.27) | copy-start | bytes 36868
  312.1 83.6 %copy-start.10 = (f32[1,1,3072]{2,1,0:T(1,128)S(1)}, f32[1,1,3072]{2,1,0:T(1,128)}, u32[]{:S(2)}) copy-start(f32[1,1,3072]{2,1,0:T(1,128)} %get-tuple-element.24) | copy-start | bytes 36868
  312.1 83.6 %copy-start.11 = (f32[1,1,3072]{2,1,0:T(1,128)S(1)}, f32[1,1,3072]{2,1,0:T(1,128)}, u32[]{:S(2)}) copy-start(f32[1,1,3072]{2,1,0:T(1,128)} %get-tuple-element.31) | copy-start | bytes 36868
  312.1 94.3 %copy-start.14 = (f32[2,64]{1,0:T(2,128)S(1)}, f32[2,64]{1,0:T(2,128)}, u32[]{:S(2)}) copy-start(f32[2,64]{1,0:T(2,128)} %param.16) | copy-start | bytes 1540
  396.0 7.5 %collective-permute-start = (f32[1,64]{1,0:T(1,128)S(1)}, f32[1,64]{1,0:T(1,128)S(1)}, u32[]{:S(2)}, u32[]{:S(2)}) collective-permute-start(f32[1,64]{1,0:T(1,128)S(1)} %get-tuple-element.45), channel_id=1, source_target_pairs={{0,1},{1,2},{2,3},{4,5},{5,6},{6,7},{8,9},{9,10},{10,11},{12,13},{... | collective-permute-start | bytes 776 | tf_op jit(solution)/shard_map/ppermute | solution.py:22
  401.5 4.9 %collective-permute-start.1 = (f32[1,64]{1,0:T(1,128)S(1)}, f32[1,64]{1,0:T(1,128)S(1)}, u32[]{:S(2)}, u32[]{:S(2)}) collective-permute-start(f32[1,64]{1,0:T(1,128)S(1)} %get-tuple-element.46), channel_id=1, source_target_pairs={{1,0},{2,1},{3,2},{5,4},{6,5},{7,6},{9,8},{10,9},{11,10},{13,12},{... | collective-permute-start | bytes 776 | tf_op jit(solution)/shard_map/ppermute | solution.py:24
Sparse Core Ops, SparseCore 0:
  101.9 42.1 all-gather.7
  146.3 43.8 all-gather.5
  192.3 79.9 all-gather.9
  321.9 72.4 all-reduce.2
where the time goes:
time: 415 us; the launch traced here: 414 us
  waiting for transfers between devices  213 us (51%)
  blocking collectives  83.5 us (20%)
  local copies, waits for them, and re-layouts  38.6 us (9%)
  other arithmetic  24.4 us (6%)
  matrix products  19.5 us (5%)
  between operations  18 us (4%)
  starting transfers between devices  16.5 us (4%)
    all_gather x1, waiting for transfers between devices, on_device(): lax.all_gather(w_out, 'row', axis=1, tiled=True)  77.3 us
    psum x1, waiting for transfers between devices, on_device(): every_sum = lax.psum(every_term, 'row')  71.4 us
    all_gather x1, waiting for transfers between devices, on_device(): value_piece = lax.all_gather(value_rows, 'row', axis=0, tiled=True)  42.3 us
    all_gather x1, blocking collectives, on_device(): lax.all_gather(normed, 'row', axis=0, tiled=True)  25.6 us
    all_gather x1, blocking collectives, on_device(): all_rows = lax.all_gather(normed_two, 'row', axis=0, tiled=True)  24.4 us
    all_gather x1, waiting for transfers between devices, on_device(): key_piece = lax.all_gather(key_rows, 'row', axis=0, tiled=True)  14.7 us
    all_to_all x1, blocking collectives, on_device(): lax.all_to_all(image_keys, 'col', split_axis=1, concat_axis=0, tiled=True)  14.5 us
    unnamed x1, blocking collectives  11.2 us
  transfers between devices with their start and end apart: 8, of which 7 were waited for; matrix products, arithmetic and copies ran while one was open for 6% of the time, Pallas kernels for 0%

commit v1 on v0

--- a/solution.py
+++ b/solution.py
@@ -1,3 +1,4 @@
+import functools
 import jax
 import jax.numpy as jnp
 from jax import lax
@@ -9,6 +10,22 @@
 eps_norm = 1e-06
 blend = 0.25
 mask_floor = -1e30
+
+
+def point_streams(array_here, link_axis):
+    dev_n = lax.axis_size(link_axis)
+    new = [(at - 1, at) for at in range(1, dev_n)] + [(dev_n - 1, 0)]
+    w2 = array_here
+    cards = [w2]
+    for _ in range(dev_n - 1):
+        w2 = lax.ppermute(w2, link_axis, new)
+        cards += [w2]
+    return jnp.roll(
+        jnp.concatenate([*reversed(cards)], 0), (lax.axis_index(link_axis) + 1) * w2.shape[0], 0
+    )
+
+
+show_targets = functools.partial(point_streams, link_axis="row")
 
 
 def with_halo(cells, sides, width):
@@ -132,7 +149,7 @@
     value_rows = jnp.concatenate([v_heads, text_values], 0)
     run_max = jnp.full((image_rows, local_heads), mask_floor, jnp.float32)
     key_piece = lax.all_gather(key_rows, "row", axis=0, tiled=True)
-    value_piece = lax.all_gather(value_rows, "row", axis=0, tiled=True)
+    value_piece = show_targets(value_rows)
     piece_rows = key_piece.shape[0]
     global_row = jnp.arange(piece_rows, dtype=jnp.int32)
     shard_id = global_row // shard_rows

time: 415 us -> 388 us (0.935)
  waiting for transfers between devices: 213 us -> 162 us
  starting transfers between devices: 16.5 us -> 30.5 us
  local copies, waits for them, and re-layouts: 38.6 us -> 45.5 us
    ppermute x0 -> x7, waiting for transfers between devices: none -> 50.2 us  [point_streams(): w2 = lax.ppermute(w2, link_axis, new)]
    all_gather x1, waiting for transfers between devices: 77.3 us -> 33.2 us  [on_device(): lax.all_gather(w_out, 'row', axis=1, tiled=True)]
    all_gather x1 -> x0, waiting for transfers between devices: 42.3 us -> none  [on_device(): value_piece = lax.all_gather(value_rows, 'row', axis=0, tiled=True)]
    all_gather x1, waiting for transfers between devices: 14.7 us -> 0.02 us  [on_device(): key_piece = lax.all_gather(key_rows, 'row', axis=0, tiled=True)]
    all_to_all x1, starting transfers between devices: 3.94 us -> 17.7 us  [on_device(): lax.all_to_all(queries, 'col', split_axis=1, concat_axis=0, tiled=True)]
    unnamed x39 -> x62, local copies, waits for them, and re-layouts: 0.96 us -> 6.11 us
    dynamic_slice x0 -> x2, local copies, waits for them, and re-layouts: none -> 4.36 us  [point_streams(): jnp.roll(jnp.concatenate([*reversed(cards)], 0), (lax.axis_index(link_axi...]
  transfers between devices with their start and end apart: 8 -> 14, of which waited for: 7 -> 11; matrix products, arithmetic and copies ran while one was open for 6% -> 8% of each run, Pallas kernels for 0% -> 0%
where the time goes in v1:
time: 388 us; the launch traced here: 386 us
  waiting for transfers between devices  162 us (42%)
  blocking collectives  83.5 us (22%)
  local copies, waits for them, and re-layouts  45.5 us (12%)
  starting transfers between devices  30.5 us (8%)
  other arithmetic  26.6 us (7%)
  matrix products  19.5 us (5%)
  between operations  18.3 us (5%)
    psum x1, waiting for transfers between devices, on_device(): every_sum = lax.psum(every_term, 'row')  71.3 us
    ppermute x7, waiting for transfers between devices, point_streams(): w2 = lax.ppermute(w2, link_axis, new)  50.2 us
    all_gather x1, waiting for transfers between devices, on_device(): lax.all_gather(w_out, 'row', axis=1, tiled=True)  33.2 us
    all_gather x1, blocking collectives, on_device(): lax.all_gather(normed, 'row', axis=0, tiled=True)  25.6 us
    all_gather x1, blocking collectives, on_device(): all_rows = lax.all_gather(normed_two, 'row', axis=0, tiled=True)  24.4 us
    all_to_all x1, starting transfers between devices, on_device(): lax.all_to_all(queries, 'col', split_axis=1, concat_axis=0, tiled=True)  17.7 us
    all_to_all x1, blocking collectives, on_device(): lax.all_to_all(image_keys, 'col', split_axis=1, concat_axis=0, tiled=True)  14.5 us
    unnamed x1, blocking collectives  11.2 us
  transfers between devices with their start and end apart: 14, of which 11 were waited for; matrix products, arithmetic and copies ran while one was open for 8% of the time, Pallas kernels for 0%

profile of v1, /device:TPU:1, one launch (start us, length us, event | category | flops | bytes accessed | tf_op | source)
XLA Modules:
  0.0 385.9 jit_solution(3877132394213461064)
XLA Ops:
  12.3 2.2 dynamic-slice_add_fusion
  15.3 25.6 %all-gather = bf16[8,2,3072]{2,1,0:T(2,128)(2,1)S(1)} all-gather(bf16[1,2,3072]{2,1,0:T(2,128)(2,1)S(1)} %fusion.50), channel_id=1, replica_groups=mesh['row'=8,'col'=4] {'row'}, dimensions={0}, use_global_device_ids=true | all-gather | bytes 110592 | tf_op jit(solution)/shard_map/all_gather | solution.py:129
  41.0 4.0 %convolution_convert_fusion.1 = bf16[16,1152]{1,0:T(8,128)(2,1)S(1)} fusion(bf16[16,3072]{1,0:T(8,128)(2,1)S(1)} %reshape.270, bf16[3072,1152]{1,0:T(8,128)(2,1)} %param.23), kind=kOutput, calls=%fused_computation.3 | convolution fusion | flops 113264640 | bytes 7213056 | tf_op jit(solution)/shard_map/dot_general | solution.py:128
  45.7 5.0 %all-to-all-start = ((bf16[8,2,1152]{2,1,0:T(2,128)(2,1)}), bf16[8,2,1152]{2,1,0:T(2,128)(2,1)S(1)}, u32[]{:S(2)}, u32[]{:S(2)}) async-start(bf16[8,2,1152]{2,1,0:T(2,128)(2,1)} %all_to_all.50), calls=%async_computation | async-start | bytes 73728 | tf_op jit(solution)/shard_map/all_to_all | solution.py:131
  59.2 2.3 reshape.264
  64.1 5.2 %slice_multiply_fusion.5 = (f32[2,24,64,1]{3,2,1,0:T(8,128)}, f32[2,24,64,1]{3,2,1,0:T(8,128)}, f32[2,24,64,1]{3,2,1,0:T(8,128)}, f32[2,24,64,1]{3,2,1,0:T(8,128...) fusion(f32[2,24,64,2]{3,2,1,0:T(8,128)S(1)} %multiply_multiply_, ...), kind=kLoop, calls=%fused_computation.11 | loop fusion | flops 24576 | bytes 148480 | tf_op jit(solution)/shard_map/mul | solution.py:86
  69.3 2.5 copy.54
  71.9 2.5 copy.55
  74.4 2.5 copy.52
  76.9 2.5 copy.53
  83.6 2.1 convert_element_type.69
  85.7 14.5 %all_to_all.67 = bf16[2,4,768]{2,0,1:T(2,128)(2,1)} all-to-all(bf16[2,4,768]{2,0,1:T(2,128)(2,1)S(1)} %copy.57), channel_id=1, replica_groups=mesh['row'=8,'col'=4] {'col'}, dimensions={1} | all-to-all | bytes 24576 | tf_op jit(solution)/shard_map/all_to_all | solution.py:141
  103.4 7.7 %all_to_all.68 = bf16[2,4,768]{2,0,1:T(2,128)(2,1)} all-to-all(bf16[2,4,768]{2,0,1:T(2,128)(2,1)} %bitcast.72), channel_id=1, replica_groups=mesh['row'=8,'col'=4] {'col'}, dimensions={1} | all-to-all | bytes 24576 | tf_op jit(solution)/shard_map/all_to_all | solution.py:142
  113.0 12.5 %collective-permute-done = bf16[136,768]{1,0:T(8,128)(2,1)S(1)} collective-permute-done((bf16[136,768]{1,0:T(8,128)(2,1)S(1)}, bf16[136,768]{1,0:T(8,128)(2,1)S(1)}, u32[]{:S(2)}, u32[]{:S(2)}) %collective-permute-start) | collective-permute-done | bytes 208928 | tf_op jit(solution)/shard_map/ppermute | solution.py:21
  126.2 9.7 %collective-permute-done.1 = bf16[136,768]{1,0:T(8,128)(2,1)S(1)} collective-permute-done((bf16[136,768]{1,0:T(8,128)(2,1)S(1)}, bf16[136,768]{1,0:T(8,128)(2,1)S(1)}, u32[]{:S(2)}, u32[]{:S(2)}) %collective-permute-start.1) | collective-permute-done | bytes 208928 | tf_op jit(solution)/shard_map/ppermute | solution.py:21
  136.6 12.0 %collective-permute-done.2 = bf16[136,768]{1,0:T(8,128)(2,1)} collective-permute-done((bf16[136,768]{1,0:T(8,128)(2,1)S(1)}, bf16[136,768]{1,0:T(8,128)(2,1)}, u32[]{:S(2)}, u32[]{:S(2)}) %collective-permute-start.2) | collective-permute-done | bytes 208928 | tf_op jit(solution)/shard_map/ppermute | solution.py:21
  149.2 2.5 copy.61
  151.8 2.5 copy.62
  157.0 7.6 %collective-permute-done.4 = bf16[136,768]{1,0:T(8,128)(2,1)S(1)} collective-permute-done((bf16[136,768]{1,0:T(8,128)(2,1)}, bf16[136,768]{1,0:T(8,128)(2,1)S(1)}, u32[]{:S(2)}, u32[]{:S(2)}) %collective-permute-start.4) | collective-permute-done | bytes 208928 | tf_op jit(solution)/shard_map/ppermute | solution.py:21
  167.4 17.7 %all-to-all-start.3 = ((bf16[2,4,768]{2,0,1:T(2,128)(2,1)}), bf16[2,4,768]{2,0,1:T(2,128)(2,1)S(1)}, u32[]{:S(2)}, u32[]{:S(2)}) async-start(bf16[2,4,768]{2,0,1:T(2,128)(2,1)} %copy.64), calls=%async_computation.3 | async-start | bytes 24576 | tf_op jit(solution)/shard_map/all_to_all | solution.py:140
  186.4 2.2 all-to-all-done.3
  188.6 8.3 %collective-permute-done.6 = bf16[136,768]{1,0:T(8,128)(2,1)S(1)} collective-permute-done((bf16[136,768]{1,0:T(8,128)(2,1)S(1)}, bf16[136,768]{1,0:T(8,128)(2,1)S(1)}, u32[]{:S(2)}, u32[]{:S(2)}) %collective-permute-start.6) | collective-permute-done | bytes 208928 | tf_op jit(solution)/shard_map/ppermute | solution.py:21
  202.6 2.7 copy.51
  205.4 3.9 %copy.58 = bf16[1088,768]{0,1:T(8,128)(2,1)} copy(bf16[1088,768]{1,0:T(8,128)(2,1)} %all-gather.5.cloned.1.call-done) | data formatting | bytes 3342336 | tf_op jit(solution)/shard_map/all_gather | solution.py:151
  211.4 33.2 %all-gather.7.cloned.1.call-done = bf16[768,3072]{1,0:T(8,128)(2,1)} async-done(((bf16[768,384]{1,0:T(8,128)(2,1)}), bf16[768,3072]{1,0:T(8,128)(2,1)}) %all-gather.7.cloned.1.call-update) | async-done | bytes 4718608 | tf_op jit(solution)/shard_map/all_gather | solution.py:189
  244.6 3.7 convolution_convert_fusion
  248.2 11.2 %all-reduce = bf16[8,3072]{1,0:T(8,128)(2,1)S(1)} all-reduce(bf16[8,3072]{1,0:T(8,128)(2,1)S(1)} %convolution_convert_fusion), channel_id=2, replica_groups=mesh['row'=8,'col'=4] {'col'}, use_global_device_ids=true, to_apply=%region_11.12.clone | all-reduce | flops 24576 | bytes 98304
  259.9 24.4 %all-gather.1 = bf16[8,2,3072]{2,1,0:T(2,128)(2,1)S(1)} all-gather(bf16[1,2,3072]{2,1,0:T(2,128)(2,1)S(1)} %fusion.51), channel_id=1, replica_groups=mesh['row'=8,'col'=4] {'row'}, dimensions={0}, use_global_device_ids=true | all-gather | bytes 110592 | tf_op jit(solution)/shard_map/all_gather | solution.py:196
  284.4 9.6 %fusion.22 = f32[16,3072]{1,0:T(8,128)} fusion(bf16[1536,3072]{1,0:T(8,128)(2,1)} %param.28, bf16[16,3072]{1,0:T(8,128)(2,1)S(1)} %reshape.272, bf16[3072,1536]{1,0:T(8,128)(2,1)} %param.27), kind=kOutput, calls=%fused_computation.37 | convolution fusion | flops 302211072 | bytes 19169280 | tf_op jit(solution)/shard_map/dot_general | solution.py:200
  295.4 71.3 %all-reduce.3.cloned.1.call-done = f32[16,3072]{1,0:T(8,128)} async-done(((f32[16,3072]{1,0:T(8,128)}), f32[16,3072]{1,0:T(8,128)}) %all-reduce.3.cloned.1.call-update) | async-done | bytes 196624 | tf_op jit(solution)/shard_map/psum | solution.py:201
  368.3 5.6 %collective-permute-start.7 = (f32[1,64]{1,0:T(1,128)S(1)}, f32[1,64]{1,0:T(1,128)S(1)}, u32[]{:S(2)}, u32[]{:S(2)}) collective-permute-start(f32[1,64]{1,0:T(1,128)S(1)} %get-tuple-element.45), channel_id=1, source_target_pairs={{0,1},{1,2},{2,3},{4,5},{5,6},{6,7},{8,9},{9,10},{10,11},{12,13},{... | collective-permute-start | bytes 776 | tf_op jit(solution)/shard_map/ppermute | solution.py:39
  375.8 2.9 collective-permute-done.8
  (149 shorter events, 45.4 us)
Async XLA Ops:
  7.2 360.8 %copy-start = (bf16[3072,64]{0,1:T(8,128)(2,1)S(1)}, bf16[3072,64]{0,1:T(8,128)(2,1)}, u32[]{:S(2)}) copy-start(bf16[3072,64]{0,1:T(8,128)(2,1)} %param.29) | copy-start | bytes 1179652
  41.0 9.8 %copy-start.15 = (s32[4,2]{0,1:T(2,128)S(1)}, s32[4,2]{0,1:T(2,128)}, u32[]{:S(2)}) copy-start(s32[4,2]{0,1:T(2,128)} %param.21) | copy-start | bytes 100
  41.0 12.2 %copy-start.18 = (f32[128]{0:T(128)S(1)}, f32[128]{0:T(128)}, u32[]{:S(2)}) copy-start(f32[128]{0:T(128)} %param.24) | copy-start | bytes 1540
  41.0 13.0 %copy-start.19 = (f32[128]{0:T(128)S(1)}, f32[128]{0:T(128)}, u32[]{:S(2)}) copy-start(f32[128]{0:T(128)} %param.25) | copy-start | bytes 1540
  45.7 10.6 %all-to-all-start = ((bf16[8,2,1152]{2,1,0:T(2,128)(2,1)}), bf16[8,2,1152]{2,1,0:T(2,128)(2,1)S(1)}, u32[]{:S(2)}, u32[]{:S(2)}) async-start(bf16[8,2,1152]{2,1,0:T(2,128)(2,1)} %all_to_all.50), calls=%async_computation | async-start | bytes 73728 | tf_op jit(solution)/shard_map/all_to_all | solution.py:131
  50.7 154.7 %all-gather.5.cloned.1.call-start = ((), (), s32[]{:S(2)}) async-start(), calls=%async_computation.4 | async-start | bytes 1880064 | tf_op jit(solution)/shard_map/all_gather | solution.py:151
  102.6 142.0 %all-gather.7.cloned.1.call-start = ((), (), s32[]{:S(2)}) async-start(), calls=%async_computation.5 | async-start | bytes 5308416 | tf_op jit(solution)/shard_map/all_gather | solution.py:189
  112.8 12.7 %collective-permute-start = (bf16[136,768]{1,0:T(8,128)(2,1)S(1)}, bf16[136,768]{1,0:T(8,128)(2,1)S(1)}, u32[]{:S(2)}, u32[]{:S(2)}) collective-permute-start(bf16[136,768]{1,0:T(8,128)(2,1)S(1)} %pad_maximum_fusion), channel_id=1, source_target_pairs={{0,4},{4,8},{8,12},{12,16},{16,20},{20,24},{24,28},{28,0},{1,5},{5... | collective-permute-start | bytes 626696 | tf_op jit(solution)/shard_map/ppermute | solution.py:21
  126.2 9.7 %collective-permute-start.1 = (bf16[136,768]{1,0:T(8,128)(2,1)S(1)}, bf16[136,768]{1,0:T(8,128)(2,1)S(1)}, u32[]{:S(2)}, u32[]{:S(2)}) collective-permute-start(bf16[136,768]{1,0:T(8,128)(2,1)S(1)} %collective-permute-done), channel_id=1, source_target_pairs={{0,4},{4,8},{8,12},{12,16},{16,20},{20,24},{24,28},{28,0},{1,5},{5... | collective-permute-start | bytes 626696 | tf_op jit(solution)/shard_map/ppermute | solution.py:21
  136.6 12.0 %collective-permute-start.2 = (bf16[136,768]{1,0:T(8,128)(2,1)S(1)}, bf16[136,768]{1,0:T(8,128)(2,1)}, u32[]{:S(2)}, u32[]{:S(2)}) collective-permute-start(bf16[136,768]{1,0:T(8,128)(2,1)S(1)} %collective-permute-done.1), channel_id=1, source_target_pairs={{0,4},{4,8},{8,12},{12,16},{16,20},{20,24},{24,28},{28,0},{1,5},{5... | collective-permute-start | bytes 626696 | tf_op jit(solution)/shard_map/ppermute | solution.py:21
  148.5 7.7 %collective-permute-start.3 = (bf16[136,768]{1,0:T(8,128)(2,1)}, bf16[136,768]{1,0:T(8,128)(2,1)}, u32[]{:S(2)}, u32[]{:S(2)}) collective-permute-start(bf16[136,768]{1,0:T(8,128)(2,1)} %collective-permute-done.2), channel_id=1, source_target_pairs={{0,4},{4,8},{8,12},{12,16},{16,20},{20,24},{24,28},{28,0},{1,5},{5... | collective-permute-start | bytes 626696 | tf_op jit(solution)/shard_map/ppermute | solution.py:21
  151.8 33.4 %copy-start.20 = (u32[32]{0:T(128)S(1)}, u32[32]{0:T(128)}, u32[]{:S(2)}) copy-start(u32[32]{0:T(128)} %constant.177) | copy-start | bytes 388
  155.4 29.7 %copy-start.11 = (s32[1088]{0:T(1024)S(1)}, s32[1088]{0:T(1024)}, u32[]{:S(2)}) copy-start(s32[1088]{0:T(1024)} %get-tuple-element.2) | copy-start | bytes 13060
  155.4 29.7 %copy-start.12 = (s32[1088]{0:T(1024)S(1)}, s32[1088]{0:T(1024)}, u32[]{:S(2)}) copy-start(s32[1088]{0:T(1024)} %get-tuple-element.3) | copy-start | bytes 13060
  155.5 43.4 %copy-start.5 = (bf16[136,768]{1,0:T(8,128)(2,1)S(1)}, bf16[136,768]{1,0:T(8,128)(2,1)}, u32[]{:S(2)}) copy-start(bf16[136,768]{1,0:T(8,128)(2,1)} %copy-done.4) | copy-start | bytes 626692
  155.5 43.4 %copy-start.3 = (bf16[136,768]{1,0:T(8,128)(2,1)S(1)}, bf16[136,768]{1,0:T(8,128)(2,1)}, u32[]{:S(2)}) copy-start(bf16[136,768]{1,0:T(8,128)(2,1)} %copy-done.2) | copy-start | bytes 626692
  155.5 43.5 %copy-start.1 = (bf16[128,768]{1,0:T(8,128)(2,1)S(1)}, bf16[128,768]{1,0:T(8,128)(2,1)}, u32[]{:S(2)}) copy-start(bf16[128,768]{1,0:T(8,128)(2,1)} %param.18) | copy-start | bytes 589828
  156.2 8.3 %collective-permute-start.4 = (bf16[136,768]{1,0:T(8,128)(2,1)}, bf16[136,768]{1,0:T(8,128)(2,1)S(1)}, u32[]{:S(2)}, u32[]{:S(2)}) collective-permute-start(bf16[136,768]{1,0:T(8,128)(2,1)} %collective-permute-done.3), channel_id=1, source_target_pairs={{0,4},{4,8},{8,12},{12,16},{16,20},{20,24},{24,28},{28,0},{1,5},{5... | collective-permute-start | bytes 626696 | tf_op jit(solution)/shard_map/ppermute | solution.py:21
  164.5 20.6 %collective-permute-start.5 = (bf16[136,768]{1,0:T(8,128)(2,1)S(1)}, bf16[136,768]{1,0:T(8,128)(2,1)S(1)}, u32[]{:S(2)}, u32[]{:S(2)}) collective-permute-start(bf16[136,768]{1,0:T(8,128)(2,1)S(1)} %collective-permute-done.4), channel_id=1, source_target_pairs={{0,4},{4,8},{8,12},{12,16},{16,20},{20,24},{24,28},{28,0},{1,5},{5... | collective-permute-start | bytes 626696 | tf_op jit(solution)/shard_map/ppermute | solution.py:21
  167.4 21.2 %all-to-all-start.3 = ((bf16[2,4,768]{2,0,1:T(2,128)(2,1)}), bf16[2,4,768]{2,0,1:T(2,128)(2,1)S(1)}, u32[]{:S(2)}, u32[]{:S(2)}) async-start(bf16[2,4,768]{2,0,1:T(2,128)(2,1)} %copy.64), calls=%async_computation.3 | async-start | bytes 24576 | tf_op jit(solution)/shard_map/all_to_all | solution.py:140
  185.1 181.6 %all-reduce.3.cloned.1.call-start = ((), (), s32[]{:S(2)}) async-start(), calls=%async_computation.6 | async-start | bytes 393216 | tf_op jit(solution)/shard_map/psum | solution.py:201
  185.1 11.8 %collective-permute-start.6 = (bf16[136,768]{1,0:T(8,128)(2,1)S(1)}, bf16[136,768]{1,0:T(8,128)(2,1)S(1)}, u32[]{:S(2)}, u32[]{:S(2)}) collective-permute-start(bf16[136,768]{1,0:T(8,128)(2,1)S(1)} %collective-permute-done.5), channel_id=1, source_target_pairs={{0,4},{4,8},{8,12},{12,16},{16,20},{20,24},{24,28},{28,0},{1,5},{5... | collective-permute-start | bytes 626696 | tf_op jit(solution)/shard_map/ppermute | solution.py:21
  244.6 14.9 %copy-start.6 = (bf16[2,3072]{1,0:T(2,128)(2,1)S(1)}, bf16[2,3072]{1,0:T(2,128)(2,1)}, u32[]{:S(2)}) copy-start(bf16[2,3072]{1,0:T(2,128)(2,1)} %param.15) | copy-start | bytes 36868
  244.6 14.9 %copy-start.10 = (f32[1,1,3072]{2,1,0:T(1,128)S(1)}, f32[1,1,3072]{2,1,0:T(1,128)}, u32[]{:S(2)}) copy-start(f32[1,1,3072]{2,1,0:T(1,128)} %get-tuple-element.30) | copy-start | bytes 36868
  244.6 15.3 %copy-start.8 = (f32[1,1,3072]{2,1,0:T(1,128)S(1)}, f32[1,1,3072]{2,1,0:T(1,128)}, u32[]{:S(2)}) copy-start(f32[1,1,3072]{2,1,0:T(1,128)} %get-tuple-element.25) | copy-start | bytes 36868
  244.6 15.3 %copy-start.9 = (f32[1,1,3072]{2,1,0:T(1,128)S(1)}, f32[1,1,3072]{2,1,0:T(1,128)}, u32[]{:S(2)}) copy-start(f32[1,1,3072]{2,1,0:T(1,128)} %get-tuple-element.26) | copy-start | bytes 36868
  284.4 82.3 %copy-start.7 = (f32[1,1,3072]{2,1,0:T(1,128)S(1)}, f32[1,1,3072]{2,1,0:T(1,128)}, u32[]{:S(2)}) copy-start(f32[1,1,3072]{2,1,0:T(1,128)} %get-tuple-element.27) | copy-start | bytes 36868
  284.4 83.6 %copy-start.13 = (f32[1,1,3072]{2,1,0:T(1,128)S(1)}, f32[1,1,3072]{2,1,0:T(1,128)}, u32[]{:S(2)}) copy-start(f32[1,1,3072]{2,1,0:T(1,128)} %get-tuple-element.24) | copy-start | bytes 36868
  284.4 83.6 %copy-start.14 = (f32[1,1,3072]{2,1,0:T(1,128)S(1)}, f32[1,1,3072]{2,1,0:T(1,128)}, u32[]{:S(2)}) copy-start(f32[1,1,3072]{2,1,0:T(1,128)} %get-tuple-element.31) | copy-start | bytes 36868
  284.4 94.3 %copy-start.17 = (f32[2,64]{1,0:T(2,128)S(1)}, f32[2,64]{1,0:T(2,128)}, u32[]{:S(2)}) copy-start(f32[2,64]{1,0:T(2,128)} %param.16) | copy-start | bytes 1540
  368.3 7.5 %collective-permute-start.7 = (f32[1,64]{1,0:T(1,128)S(1)}, f32[1,64]{1,0:T(1,128)S(1)}, u32[]{:S(2)}, u32[]{:S(2)}) collective-permute-start(f32[1,64]{1,0:T(1,128)S(1)} %get-tuple-element.45), channel_id=1, source_target_pairs={{0,1},{1,2},{2,3},{4,5},{5,6},{6,7},{8,9},{9,10},{10,11},{12,13},{... | collective-permute-start | bytes 776 | tf_op jit(solution)/shard_map/ppermute | solution.py:39
  373.8 4.9 %collective-permute-start.8 = (f32[1,64]{1,0:T(1,128)S(1)}, f32[1,64]{1,0:T(1,128)S(1)}, u32[]{:S(2)}, u32[]{:S(2)}) collective-permute-start(f32[1,64]{1,0:T(1,128)S(1)} %get-tuple-element.46), channel_id=1, source_target_pairs={{1,0},{2,1},{3,2},{5,4},{6,5},{7,6},{9,8},{10,9},{11,10},{13,12},{... | collective-permute-start | bytes 776 | tf_op jit(solution)/shard_map/ppermute | solution.py:41
  (3 other events, 11.2 us)
Sparse Core Ops, SparseCore 0:
  102.7 49.8 all-gather.4
  154.7 89.8 all-gather.6
  294.2 72.4 all-reduce.2
